TPU v7x, 256 devices: a whole 4x4x8 slice. The times are simulated.
256 devices in a mesh: ctx: 32 (over x, y, core), head: 8 (over z).
Axes of the slice: x: 4, y: 4, z: 8, core: 2. Of those that a mesh axis runs over, the one named last changes fastest.
Arguments:
- lin_q: bfloat16 [8192, 8192], P('ctx', 'head'), may hold values from -4 to 4
- lin_k: bfloat16 [8192, 8192], P('ctx', 'head'), may hold values from -4 to 4
- lin_v: bfloat16 [8192, 8192], P('ctx', 'head'), may hold values from -6 to 6
- log_decay: float32 [64, 8192], P('head', 'ctx'), may hold values from -1 to 0
- lin_gain: float32 [8192], P('head'), may hold values from 0.1 to 1.9
- soft_q: bfloat16 [8192, 8192], P(('ctx', 'head')), may hold values from -200 to 200
- soft_kv: bfloat16 [8192, 2048], P(('ctx', 'head')), may hold values from -8 to 8
Outputs:
- lin_out: bfloat16 [8192, 8192], P('ctx', 'head')
- soft_out: bfloat16 [8192, 8192], P(('ctx', 'head'))
All inputs are finite; a program needn't handle non-finite values.
Results may differ from a plain program's by a relative error of at most 0.013.
Values may be sent and summed in bfloat16 or wider, within the bound.
No kernel may reach another device: no remote copies, remote signals or barrier semaphores. Data moves between devices by JAX's collectives and lax.ppermute only.
A program may use at most 64 MiB of HBM per device.

v0:
```python
import math
import jax
import jax.numpy as jnp
from jax import lax
from jax.sharding import Mesh
from jax.sharding import PartitionSpec as P

CTX = ("ctx_0", "ctx_1", "ctx_2")
CTX_HEAD = ("ctx_0", "ctx_1", "ctx_2", "head")


def filled_with(value, identity):
    return jax.tree.map(
        lambda part, zero: jnp.zeros_like(part) + jnp.asarray(zero, part.dtype), value, identity
    )


def carried_in(value, axes, combine, identity):
    before = start = filled_with(value, identity)
    so_far = value
    for axis in reversed(axes):
        devices, index = (lax.axis_size(axis), lax.axis_index(axis))
        pieces = jax.tree.map(
            lambda part, kind: lax.all_gather(part.astype(kind), axis),
            so_far,
            (jnp.bfloat16, jnp.bfloat16),
        )
        inside, so_far = (start, start)
        for k in range(devices):
            passed = k < index
            so_far = combine(
                so_far, jax.tree.map(lambda part, own: part[k].astype(own.dtype), pieces, value)
            )
            inside = jax.tree.map(lambda new, old: jnp.where(passed, new, old), so_far, inside)
        before = combine(inside, before)
    return before


def block_local(kb, gb):
    cum = jnp.cumsum(gb, axis=1)
    keys_scaled = (kb.astype(jnp.float32) * jnp.exp(cum[:, -1:] - cum).T[:, :, None]).astype(
        jnp.bfloat16
    )
    return (cum, keys_scaled)


def block_output(qb, kb, vb, cum, state):
    size = cum.shape[1]
    pos = jnp.arange(size)
    causal = pos[:, None] >= pos[None, :]
    diff = cum[:, :, None] - cum[:, None, :]
    weight = jnp.where(causal[None], jnp.exp(jnp.minimum(diff, 0.0)), 0.0)
    scores = jnp.einsum("thd,shd->hts", qb, kb, preferred_element_type=jnp.float32)
    probs = (scores * weight).astype(jnp.bfloat16)
    intra = jnp.einsum("hts,shd->thd", probs, vb, preferred_element_type=jnp.float32)
    inter = jnp.einsum(
        "thd,hde->the", qb, state.astype(jnp.bfloat16), preferred_element_type=jnp.float32
    )
    return intra + jnp.exp(cum).T[:, :, None] * inter


def join_states(earlier, later):
    return (earlier[0] + later[0], jnp.exp(later[0])[:, None, None] * earlier[1] + later[1])


def lightning_part(lin_q, lin_k, lin_v, log_decay, lin_gain):
    tok, width = lin_q.shape
    heads = log_decay.shape[0]
    dim = width // heads
    q = lin_q.reshape(tok, heads, dim)
    k = lin_k.reshape(tok, heads, dim)
    v = lin_v.reshape(tok, heads, dim)
    total = (jnp.zeros((heads,), jnp.float32), jnp.zeros((heads, dim, dim), jnp.float32))
    cum, keys_scaled = block_local(k, log_decay)
    local = jnp.einsum("shd,she->hde", keys_scaled, v, preferred_element_type=jnp.float32)
    total = join_states(total, (cum[:, -1], local))
    identity = (jnp.zeros((heads,), jnp.float32), jnp.zeros((heads, dim, dim), jnp.float32))
    entering = carried_in((total[0], total[1]), CTX, join_states, identity)
    state = entering[1]
    mixed = block_output(q, k, v, cum, state)
    rms = jnp.sqrt(jnp.mean(mixed * mixed, axis=-1, keepdims=True) + 1e-05)
    outputs = mixed / rms * lin_gain.reshape(heads, dim)
    return outputs.reshape(tok, width).astype(jnp.bfloat16)


def softmax_part(soft_q, soft_kv, dim):
    local_q, local_kv = (
        lax.all_to_all(soft_q, "head", split_axis=1, concat_axis=0, tiled=True),
        lax.all_to_all(soft_kv, "head", split_axis=1, concat_axis=0, tiled=True),
    )
    tok = local_q.shape[0]
    half = tok // 2
    kvl = local_kv.shape[1] // (2 * dim)
    group = local_q.shape[1] // (dim * kvl)
    mine = lax.axis_index(CTX)
    first_q = local_q[:half]
    second_q = local_q[half:]
    second_start = mine * tok + half
    first_start = mine * tok
    first_pos = first_start + jnp.arange(half)
    second_pos = second_start + jnp.arange(half)
    first_heads = first_q.reshape(half, kvl, group, dim)
    second_heads = second_q.reshape(half, kvl, group, dim)
    scale = dim ** (-0.5)

    def update(carry, queries, qpos, kblock, kstart):
        peak, total, acc = carry
        size = kblock.shape[0]
        pair = kblock.reshape(size, kvl, 2, dim)
        key_matrix = pair[:, :, 0]
        value_rows = pair[:, :, 1]
        kpos = kstart + jnp.arange(size)
        mask = (kpos[None, :] <= qpos[:, None])[None, None]
        scores = (
            jnp.einsum("qngd,knd->ngqk", queries, key_matrix, preferred_element_type=jnp.float32)
            * scale
        )
        scores = jnp.where(mask, scores, -1e30)
        newpeak = jnp.maximum(peak, jnp.max(scores, axis=-1))
        weights = jnp.where(mask, jnp.exp(scores - newpeak[..., None]), 0.0)
        decay_factor = jnp.exp(peak - newpeak)
        total = total * decay_factor + jnp.sum(weights, axis=-1)
        acc = acc * decay_factor[..., None] + jnp.einsum(
            "ngqk,knd->ngqd",
            weights.astype(jnp.bfloat16),
            value_rows,
            preferred_element_type=jnp.float32,
        )
        return (newpeak, total, acc)

    def guarded(carry, queries, qpos, qlast, kblock, kstart):
        return lax.cond(
            kstart <= qlast, lambda c: update(c, queries, qpos, kblock, kstart), lambda c: c, carry
        )

    def start_carry():
        return (
            jnp.full((kvl, group, half), -1e30, jnp.float32),
            jnp.zeros((kvl, group, half), jnp.float32),
            jnp.zeros((kvl, group, half, dim), jnp.float32),
        )

    def finish(carry):
        peak, total, acc = carry
        result = acc / total[..., None]
        return result.transpose(2, 0, 1, 3).reshape(half, kvl * group * dim).astype(jnp.bfloat16)

    piece = lax.all_gather(local_kv, CTX, axis=0, tiled=True)
    rows = piece.shape[0]
    width = math.gcd(rows, 512)

    def step(index, inner):
        kblock = lax.dynamic_slice_in_dim(piece, index * width, width, 0)
        kstart = index * width
        early = guarded(inner[0], first_heads, first_pos, first_start + half - 1, kblock, kstart)
        later = guarded(inner[1], second_heads, second_pos, second_start + half - 1, kblock, kstart)
        return (early, later)

    early, later = lax.fori_loop(0, rows // width, step, (start_carry(), start_carry()))
    first_out = finish(early)
    second_out = finish(later)
    result = jnp.concatenate([first_out, second_out], axis=0)
    return lax.all_to_all(result, "head", split_axis=0, concat_axis=1, tiled=True)


def body(lin_q, lin_k, lin_v, log_decay, lin_gain, soft_q, soft_kv):
    heads = log_decay.shape[0]
    dim = lin_q.shape[1] // heads
    lin_out = lightning_part(lin_q, lin_k, lin_v, log_decay, lin_gain)
    soft_out = softmax_part(soft_q, soft_kv, dim)
    return (lin_out, soft_out)


def solution(mesh):
    finer = Mesh(
        mesh.devices.reshape(4, 4, 2, mesh.shape["head"]), ("ctx_0", "ctx_1", "ctx_2", "head")
    )
    placed = (
        P(CTX, "head"),
        P(CTX, "head"),
        P(CTX, "head"),
        P("head", CTX),
        P("head"),
        P(CTX_HEAD, None),
        P(CTX_HEAD, None),
    )
    return jax.shard_map(
        body,
        mesh=finer,
        in_specs=placed,
        out_specs=(P(CTX, "head"), P(CTX_HEAD, None)),
        check_vma=False,
    )
```

profile of v0, /device:TPU:31, one launch (start us, length us, event | category | flops | bytes accessed | tf_op | source)
XLA Modules:
  0.0 221.1 jit_solution(15442327545542827741)
XLA Ops:
  11.4 2.8 %all-reduce = bf16[16]{0:T(256)(128)(2,1)S(1)} all-reduce(bf16[16]{0:T(256)(128)(2,1)S(1)} %dynamic-update-slice), channel_id=2, replica_groups=mesh['ctx_0'=4,'ctx_1'=4,'ctx_2'=2,'head'=8] {'ctx_2'}, use_global_device_ids=true, to_apply=%add | all-reduce | flops 16 | bytes 64
  17.7 2.2 all-gather.1
  20.9 16.0 %all_to_all.54 = bf16[32,8,256]{2,0,1:T(8,128)(2,1)} all-to-all(bf16[32,8,256]{2,0,1:T(8,128)(2,1)S(1)} %bitcast.354), channel_id=1, replica_groups=mesh['ctx_0'=4,'ctx_1'=4,'ctx_2'=2,'head'=8] {'head'}, dimensions={1} | all-to-all | bytes 262144 | tf_op jit(solution)/shard_map/all_to_all | solution.py:89
  37.8 3.5 %all-to-all-start.1 = ((bf16[32,8,1024]{2,0,1:T(8,128)(2,1)}), bf16[32,8,1024]{2,0,1:T(8,128)(2,1)S(1)}, u32[]{:S(2)}, u32[]{:S(2)}) async-start(bf16[32,8,1024]{2,0,1:T(8,128)(2,1)} %bitcast.330), calls=%async_computation.1 | async-start | bytes 1048576 | tf_op jit(solution)/shard_map/all_to_all | solution.py:88
  41.4 5.2 %all-gather.2 = bf16[4,1,8]{2,1,0:T(2,128)(2,1)S(1)} all-gather(bf16[1,1,8]{2,1,0:T(2,128)(2,1)S(1)} %get-tuple-element.626), channel_id=1, replica_groups=mesh['ctx_0'=4,'ctx_1'=4,'ctx_2'=2,'head'=8] {'ctx_1'}, dimensions={0}, use_global_device_ids=true | all-gather | bytes 80 | tf_op jit(solution)/shard_map/all_gather | solution.py:24
  46.6 5.3 %all-gather.3 = bf16[4,1,8]{2,1,0:T(2,128)(2,1)S(1)} all-gather(bf16[1,1,8]{2,1,0:T(2,128)(2,1)S(1)} %get-tuple-element.620), channel_id=1, replica_groups=mesh['ctx_0'=4,'ctx_1'=4,'ctx_2'=2,'head'=8] {'ctx_0'}, dimensions={0}, use_global_device_ids=true | all-gather | bytes 80 | tf_op jit(solution)/shard_map/all_gather | solution.py:24
  52.0 5.0 %all-to-all-done.1 = bf16[32,8,1024]{2,0,1:T(8,128)(2,1)S(1)} async-done(((bf16[32,8,1024]{2,0,1:T(8,128)(2,1)}), bf16[32,8,1024]{2,0,1:T(8,128)(2,1)S(1)}, u32[]{:S(2)}, u32[]{:S(2)}) %all-to-all-start.1) | async-done | bytes 524320 | tf_op jit(solution)/shard_map/all_to_all | solution.py:88
  57.3 2.3 %fusion.66 = bf16[1,8,128,128]{3,2,1,0:T(8,128)(2,1)} fusion(f32[8]{0:T(128)S(1)} %get-tuple-element.624, f32[8]{0:T(128)S(1)} %get-tuple-element.623, f32[8]{0:T(128)S(1)} %get-tuple-element.622, f32[8]{0:T(128)S(1)} %get-tuple-element.621, bf16[4,8,128,128]{3,2,1,0:T(8,128)(2,1)} %all-gather.8.cloned.1.call-done), kind=kLoop, calls=%fused_computation.103 | loop fusion | flops 1572864 | bytes 1310848 | tf_op jit(solution)/shard_map/convert_element_type | solution.py:24
  59.6 42.5 %all-gather.12.cloned.1.call-done = bf16[8192,256]{1,0:T(8,128)(2,1)} async-done(((bf16[256,256]{1,0:T(8,128)(2,1)}), bf16[8192,256]{1,0:T(8,128)(2,1)}) %all-gather.12.cloned.1.call-update) | async-done | bytes 4194320 | tf_op jit(solution)/shard_map/all_gather | solution.py:148
  102.3 85.3 %while.27 = (s32[]{:T(128)}, f32[1,8,128]{2,1,0:T(8,128)S(1)}, f32[1,8,128]{2,1,0:T(8,128)S(1)}, f32[1,8,128,128]{3,2,1,0:T(8,128)S(1)}, f32[1,8,128]{2,1,0:T(8,...) while((s32[]{:T(128)}, f32[1,8,128]{2,1,0:T(8,128)S(1)}, ...), condition=%wide.region_12.13_spmd.clone, body=%wide.region_3.12_spmd.clone.sunk | while | flops 551165184 | bytes 17445364 | solution.py:159
  130.1 2.1 conditional.7
  135.4 2.1 conditional.7
  140.7 2.1 conditional.7
  146.1 2.1 conditional.7
  151.4 2.1 conditional.7
  156.7 2.1 conditional.7
  162.0 2.1 conditional.7
  167.4 2.1 conditional.7
  172.7 2.1 conditional.7
  178.0 2.1 conditional.7
  189.2 6.7 %all-to-all-start.2 = ((bf16[8,32,1024]{2,1,0:T(8,128)(2,1)}), bf16[8,32,1024]{2,1,0:T(8,128)(2,1)S(1)}, u32[]{:S(2)}, u32[]{:S(2)}) async-start(bf16[8,32,1024]{2,1,0:T(8,128)(2,1)} %bitcast.73), calls=%async_computation.2 | async-start | bytes 1048576 | tf_op jit(solution)/shard_map/all_to_all | solution.py:163
  195.9 3.6 %fusion.41 = f32[256,8,128]{0,2,1:T(8,128)} fusion(f32[256,8]{0,1:T(8,128)S(1)} %get-tuple-element.608, bf16[4,8,128,128]{3,2,1,0:T(8,128)(2,1)} %all-gather.10.cloned.1.call-done, f32[8]{0:T(128)S(1)} %get-tuple-element.627, f32[8]{0:T(128)S(1)} %get-tuple-element.625, f32[8]{0:T(128)S(1)} %get-tuple-element.624, f32[8]{0:T(128)S(1)} %get-tuple-element.623, ...), kind=kOutput, calls=%fused_computation.62 | convolution fusion | flops 72876032 | bytes 4202890 | tf_op jit(solution)/shard_map/thd,hde->the/dot_general | solution.py:56
  199.5 2.4 %multiply_reduce_fusion = (f32[256,8]{0,1:T(8,128)S(1)}, f32[256,8,128]{0,2,1:T(8,128)S(1)}) fusion(f32[256,8,128]{0,2,1:T(8,128)} %fusion.41, bf16[256,8,128]{0,2,1:T(8,128)(2,1)S(1)} %bitcast.351, f32[8,256]{1,0:T(8,128)S(1)} %get-tuple-element.609, pred[256,256]{1,0:T(8,128)(4,1)S(1)} %iota_compare_fusion, bf16[256,1024]{1,0:T(8,128)(2,1)} %param.15, ...), kind=kOutput, calls=%fused_computation.66 | convolution fusion | flops 271841280 | bytes 3751936 | tf_op jit(solution)/shard_map/hts,shd->thd/dot_general | solution.py:55
  203.1 10.7 %all-to-all-done.2 = bf16[8,32,1024]{2,1,0:T(8,128)(2,1)S(1)} async-done(((bf16[8,32,1024]{2,1,0:T(8,128)(2,1)}), bf16[8,32,1024]{2,1,0:T(8,128)(2,1)S(1)}, u32[]{:S(2)}, u32[]{:S(2)}) %all-to-all-start.2) | async-done | bytes 524320 | tf_op jit(solution)/shard_map/all_to_all | solution.py:163
  (438 shorter events, 139.9 us)
Async XLA Ops:
  7.2 188.7 %copy-start = (bf16[256,1024]{1,0:T(8,128)(2,1)S(1)}, bf16[256,1024]{1,0:T(8,128)(2,1)}, u32[]{:S(2)}) copy-start(bf16[256,1024]{1,0:T(8,128)(2,1)} %param.13) | copy-start | bytes 1572868
  7.2 50.1 %all-gather.8.cloned.1.call-start = ((), (), s32[]{:S(2)}) async-start(), calls=%async_computation.3 | async-start | bytes 1310720 | tf_op jit(solution)/shard_map/all_gather | solution.py:24
  14.3 6.6 %copy-start.4 = (bf16[32,2048]{1,0:T(8,128)(2,1)S(1)}, bf16[32,2048]{1,0:T(8,128)(2,1)}, u32[]{:S(2)}) copy-start(bf16[32,2048]{1,0:T(8,128)(2,1)} %param.19) | copy-start | bytes 393220
  15.6 0.8 copy-start.2
  15.6 21.4 %copy-start.1 = (bf16[32,8192]{1,0:T(8,128)(2,1)S(1)}, bf16[32,8192]{1,0:T(8,128)(2,1)}, u32[]{:S(2)}) copy-start(bf16[32,8192]{1,0:T(8,128)(2,1)} %param.18) | copy-start | bytes 1572868
  20.8 81.3 %all-gather.12.cloned.1.call-start = ((), (), s32[]{:S(2)}) async-start(), calls=%async_computation.5 | async-start | bytes 4325376 | tf_op jit(solution)/shard_map/all_gather | solution.py:148
  37.8 19.2 %all-to-all-start.1 = ((bf16[32,8,1024]{2,0,1:T(8,128)(2,1)}), bf16[32,8,1024]{2,0,1:T(8,128)(2,1)S(1)}, u32[]{:S(2)}, u32[]{:S(2)}) async-start(bf16[32,8,1024]{2,0,1:T(8,128)(2,1)} %bitcast.330), calls=%async_computation.1 | async-start | bytes 1048576 | tf_op jit(solution)/shard_map/all_to_all | solution.py:88
  41.3 154.5 %all-gather.10.cloned.1.call-start = ((), (), s32[]{:S(2)}) async-start(), calls=%async_computation.4 | async-start | bytes 1310720 | tf_op jit(solution)/shard_map/all_gather | solution.py:24
  189.2 24.6 %all-to-all-start.2 = ((bf16[8,32,1024]{2,1,0:T(8,128)(2,1)}), bf16[8,32,1024]{2,1,0:T(8,128)(2,1)S(1)}, u32[]{:S(2)}, u32[]{:S(2)}) async-start(bf16[8,32,1024]{2,1,0:T(8,128)(2,1)} %bitcast.73), calls=%async_computation.2 | async-start | bytes 1048576 | tf_op jit(solution)/shard_map/all_to_all | solution.py:163
  195.9 3.6 %copy-start.3 = (bf16[256,1024]{0,1:T(8,128)(2,1)S(1)}, bf16[256,1024]{0,1:T(8,128)(2,1)}, u32[]{:S(2)}) copy-start(bf16[256,1024]{0,1:T(8,128)(2,1)} %copy-done.2) | copy-start | bytes 1572868
  199.5 2.4 %copy-start.5 = (f32[1024]{0:T(1024)S(1)}, f32[1024]{0:T(1024)}, u32[]{:S(2)}) copy-start(f32[1024]{0:T(1024)} %param.17) | copy-start | bytes 12292
Sparse Core Ops, SparseCore 0:
  20.9 26.1 all-gather.7
  49.7 52.4 all-gather.11
  104.5 25.1 all-gather.9
where the time goes:
time: 222 us; the launch traced here: 221 us
  waiting for transfers between devices  58.3 us (26%)
  matrix products  49.3 us (22%)
  blocking collectives  31.5 us (14%)
  other arithmetic  26.8 us (12%)
  local copies, waits for them, and re-layouts  26.5 us (12%)
  between operations  14.7 us (7%)
  starting transfers between devices  10.3 us (5%)
  loops' own time  3.78 us (2%)
    all_gather x1, waiting for transfers between devices, softmax_part(): piece = lax.all_gather(local_kv, CTX, axis=0, tiled=True)  42.5 us
    dot_general x32, matrix products, update(): jnp.einsum('ngqk,knd->ngqd', weights.astype(jnp.bfloat16), value_rows, pr...  26.6 us
    dynamic_slice x32, local copies, waits for them, and re-layouts, step(): kblock = lax.dynamic_slice_in_dim(piece, index * width, width, 0)  17.8 us
    reduce_sum x32, other arithmetic, update(): total = total * decay_factor + jnp.sum(weights, axis=-1)  16.4 us
    all_to_all x1, blocking collectives, softmax_part(): lax.all_to_all(soft_kv, 'head', split_axis=1, concat_axis=0, tiled=True)  16 us
    dot_general x32, matrix products, update(): jnp.einsum('qngd,knd->ngqk', queries, key_matrix, preferred_element_type=...  15.3 us
    all_gather x3, blocking collectives, carried_in(): lax.all_gather(part.astype(kind), axis)  12.7 us
    all_to_all x1, waiting for transfers between devices, softmax_part(): lax.all_to_all(result, 'head', split_axis=0, concat_axis=1, tiled=True)  10.7 us
  transfers between devices with their start and end apart: 5, of which 3 were waited for; matrix products, arithmetic and copies ran while one was open for 42% of the time, Pallas kernels for 0%

commit v1 on v0

--- a/solution.py
+++ b/solution.py
@@ -145,7 +145,8 @@
         result = acc / total[..., None]
         return result.transpose(2, 0, 1, 3).reshape(half, kvl * group * dim).astype(jnp.bfloat16)
 
-    piece = lax.all_gather(local_kv, CTX, axis=0, tiled=True)
+    outgoing = jnp.stack([local_kv] * lax.axis_size(CTX))
+    piece = jnp.concatenate(lax.all_to_all(outgoing, CTX, 0, 0), axis=0)
     rows = piece.shape[0]
     width = math.gcd(rows, 512)
 

time: 222 us -> 244 us (1.099)
  the two profiles are of different devices: /device:TPU:31 before, /device:TPU:30 now
where the time goes in v1:
time: 244 us; the launch traced here: 243 us
  blocking collectives  60.1 us (25%)
  matrix products  48.3 us (20%)
  local copies, waits for them, and re-layouts  35.6 us (15%)
  waiting for transfers between devices  30.7 us (13%)
  other arithmetic  26.1 us (11%)
  starting transfers between devices  23 us (9%)
  between operations  15 us (6%)
  loops' own time  3.77 us (2%)
    all_gather x3, blocking collectives, carried_in(): lax.all_gather(part.astype(kind), axis)  57.6 us
    dot_general x32, matrix products, update(): jnp.einsum('ngqk,knd->ngqd', weights.astype(jnp.bfloat16), value_rows, pr...  26.7 us
    dynamic_slice x32, local copies, waits for them, and re-layouts, step(): kblock = lax.dynamic_slice_in_dim(piece, index * width, width, 0)  17.8 us
    reduce_sum x32, other arithmetic, update(): total = total * decay_factor + jnp.sum(weights, axis=-1)  16.4 us
    all_to_all x1, waiting for transfers between devices, softmax_part(): lax.all_to_all(soft_q, 'head', split_axis=1, concat_axis=0, tiled=True)  16 us
    dot_general x32, matrix products, update(): jnp.einsum('qngd,knd->ngqk', queries, key_matrix, preferred_element_type=...  15.3 us
    all_to_all x1, starting transfers between devices, softmax_part(): lax.all_to_all(soft_kv, 'head', split_axis=1, concat_axis=0, tiled=True)  8.47 us
    all_to_all x1, starting transfers between devices, softmax_part(): piece = jnp.concatenate(lax.all_to_all(outgoing, CTX, 0, 0), axis=0)  7.5 us
  transfers between devices with their start and end apart: 6, of which 3 were waited for; matrix products, arithmetic and copies ran while one was open for 43% of the time, Pallas kernels for 0%

profile of v1, /device:TPU:30, one launch (start us, length us, event | category | flops | bytes accessed | tf_op | source)
XLA Modules:
  0.0 242.6 jit_solution(10323055746601569506)
XLA Ops:
  8.8 8.5 %all-to-all-start = ((bf16[32,8,256]{2,0,1:T(8,128)(2,1)}), bf16[32,8,256]{2,0,1:T(8,128)(2,1)S(1)}, u32[]{:S(2)}, u32[]{:S(2)}) async-start(bf16[32,8,256]{2,0,1:T(8,128)(2,1)} %bitcast.332), calls=%async_computation | async-start | bytes 262144 | tf_op jit(solution)/shard_map/all_to_all | solution.py:89
  19.1 7.2 %all-to-all-done = bf16[32,8,256]{2,0,1:T(8,128)(2,1)S(1)} async-done(((bf16[32,8,256]{2,0,1:T(8,128)(2,1)}), bf16[32,8,256]{2,0,1:T(8,128)(2,1)S(1)}, u32[]{:S(2)}, u32[]{:S(2)}) %all-to-all-start) | async-done | bytes 131104 | tf_op jit(solution)/shard_map/all_to_all | solution.py:89
  26.4 3.5 %all-to-all-start.2 = ((bf16[32,8,1024]{2,0,1:T(8,128)(2,1)}), bf16[32,8,1024]{2,0,1:T(8,128)(2,1)S(1)}, u32[]{:S(2)}, u32[]{:S(2)}) async-start(bf16[32,8,1024]{2,0,1:T(8,128)(2,1)} %bitcast.331), calls=%async_computation.2 | async-start | bytes 1048576 | tf_op jit(solution)/shard_map/all_to_all | solution.py:88
  30.0 16.0 %all-to-all-done.2 = bf16[32,8,1024]{2,0,1:T(8,128)(2,1)S(1)} async-done(((bf16[32,8,1024]{2,0,1:T(8,128)(2,1)}), bf16[32,8,1024]{2,0,1:T(8,128)(2,1)S(1)}, u32[]{:S(2)}, u32[]{:S(2)}) %all-to-all-start.2) | async-done | bytes 524320 | tf_op jit(solution)/shard_map/all_to_all | solution.py:88
  45.9 2.4 stack.5
  48.4 7.5 %all-to-all-start.1 = ((bf16[32,256,256]{1,2,0:T(8,128)(2,1)}), bf16[32,256,256]{1,2,0:T(8,128)(2,1)}, u32[]{:S(2)}, u32[]{:S(2)}) async-start(bf16[32,256,256]{1,2,0:T(8,128)(2,1)} %stack.5), calls=%async_computation.1 | async-start | bytes 8388608 | tf_op jit(solution)/shard_map/all_to_all | solution.py:149
  58.5 2.4 %all-reduce = bf16[16]{0:T(256)(128)(2,1)S(1)} all-reduce(bf16[16]{0:T(256)(128)(2,1)S(1)} %dynamic-update-slice), channel_id=2, replica_groups=mesh['ctx_0'=4,'ctx_1'=4,'ctx_2'=2,'head'=8] {'ctx_2'}, use_global_device_ids=true, to_apply=%add | all-reduce | flops 16 | bytes 64
  61.7 2.2 all-gather.1
  65.0 48.7 %all-gather.2 = bf16[4,1,8]{2,1,0:T(2,128)(2,1)S(1)} all-gather(bf16[1,1,8]{2,1,0:T(2,128)(2,1)S(1)} %get-tuple-element.626), channel_id=1, replica_groups=mesh['ctx_0'=4,'ctx_1'=4,'ctx_2'=2,'head'=8] {'ctx_1'}, dimensions={0}, use_global_device_ids=true | all-gather | bytes 80 | tf_op jit(solution)/shard_map/all_gather | solution.py:24
  113.8 6.7 %all-gather.3 = bf16[4,1,8]{2,1,0:T(2,128)(2,1)S(1)} all-gather(bf16[1,1,8]{2,1,0:T(2,128)(2,1)S(1)} %get-tuple-element.620), channel_id=1, replica_groups=mesh['ctx_0'=4,'ctx_1'=4,'ctx_2'=2,'head'=8] {'ctx_0'}, dimensions={0}, use_global_device_ids=true | all-gather | bytes 80 | tf_op jit(solution)/shard_map/all_gather | solution.py:24
  120.8 2.3 fusion.66
  123.2 6.4 %copy.101 = bf16[32,256,256]{2,1,0:T(8,128)(2,1)} copy(bf16[32,256,256]{1,2,0:T(8,128)(2,1)} %all-to-all-done.1) | data formatting | bytes 8388608 | tf_op jit(solution)/shard_map/all_to_all | solution.py:149
  129.7 85.3 %while.27 = (s32[]{:T(128)}, f32[1,8,128]{2,1,0:T(8,128)S(1)}, f32[1,8,128]{2,1,0:T(8,128)S(1)}, f32[1,8,128,128]{3,2,1,0:T(8,128)S(1)}, f32[1,8,128]{2,1,0:T(8,...) while((s32[]{:T(128)}, f32[1,8,128]{2,1,0:T(8,128)S(1)}, ...), condition=%wide.region_12.13_spmd.clone, body=%wide.region_3.12_spmd.clone.sunk | while | flops 551165184 | bytes 17445364 | solution.py:160
  130.9 2.1 conditional.7
  152.2 2.1 conditional.7
  157.5 2.1 conditional.7
  173.5 2.1 conditional.7
  178.8 2.1 conditional.7
  194.8 2.1 conditional.7
  200.2 2.1 conditional.7
  216.6 3.5 %all-to-all-start.3 = ((bf16[8,32,1024]{2,1,0:T(8,128)(2,1)}), bf16[8,32,1024]{2,1,0:T(8,128)(2,1)S(1)}, u32[]{:S(2)}, u32[]{:S(2)}) async-start(bf16[8,32,1024]{2,1,0:T(8,128)(2,1)} %bitcast.74), calls=%async_computation.3 | async-start | bytes 1048576 | tf_op jit(solution)/shard_map/all_to_all | solution.py:164
  220.2 3.6 %fusion.41 = f32[256,8,128]{0,2,1:T(8,128)} fusion(f32[256,8]{0,1:T(8,128)S(1)} %get-tuple-element.608, bf16[4,8,128,128]{3,2,1,0:T(8,128)(2,1)} %all-gather.9.cloned.1.call-done, f32[8]{0:T(128)S(1)} %get-tuple-element.627, f32[8]{0:T(128)S(1)} %get-tuple-element.625, f32[8]{0:T(128)S(1)} %get-tuple-element.624, f32[8]{0:T(128)S(1)} %get-tuple-element.623, ...), kind=kOutput, calls=%fused_computation.62 | convolution fusion | flops 72876032 | bytes 4202890 | tf_op jit(solution)/shard_map/thd,hde->the/dot_general | solution.py:56
  223.8 2.4 multiply_reduce_fusion
  227.4 7.5 %all-to-all-done.3 = bf16[8,32,1024]{2,1,0:T(8,128)(2,1)S(1)} async-done(((bf16[8,32,1024]{2,1,0:T(8,128)(2,1)}), bf16[8,32,1024]{2,1,0:T(8,128)(2,1)S(1)}, u32[]{:S(2)}, u32[]{:S(2)}) %all-to-all-start.3) | async-done | bytes 524320 | tf_op jit(solution)/shard_map/all_to_all | solution.py:164
  (445 shorter events, 144.6 us)
Async XLA Ops:
  7.2 213.0 %copy-start = (bf16[256,1024]{1,0:T(8,128)(2,1)S(1)}, bf16[256,1024]{1,0:T(8,128)(2,1)}, u32[]{:S(2)}) copy-start(bf16[256,1024]{1,0:T(8,128)(2,1)} %param.13) | copy-start | bytes 1572868
  8.8 17.6 %all-to-all-start = ((bf16[32,8,256]{2,0,1:T(8,128)(2,1)}), bf16[32,8,256]{2,0,1:T(8,128)(2,1)S(1)}, u32[]{:S(2)}, u32[]{:S(2)}) async-start(bf16[32,8,256]{2,0,1:T(8,128)(2,1)} %bitcast.332), calls=%async_computation | async-start | bytes 262144 | tf_op jit(solution)/shard_map/all_to_all | solution.py:89
  26.4 19.6 %all-to-all-start.2 = ((bf16[32,8,1024]{2,0,1:T(8,128)(2,1)}), bf16[32,8,1024]{2,0,1:T(8,128)(2,1)S(1)}, u32[]{:S(2)}, u32[]{:S(2)}) async-start(bf16[32,8,1024]{2,0,1:T(8,128)(2,1)} %bitcast.331), calls=%async_computation.2 | async-start | bytes 1048576 | tf_op jit(solution)/shard_map/all_to_all | solution.py:88
  48.3 7.6 %copy-start.4 = (f32[8,256]{1,0:T(8,128)S(1)}, f32[8,256]{1,0:T(8,128)}, u32[]{:S(2)}) copy-start(f32[8,256]{1,0:T(8,128)} %param.16) | copy-start | bytes 24580
  48.4 8.4 %copy-start.7 = (u32[256]{0:T(256)S(1)}, u32[256]{0:T(256)}, u32[]{:S(2)}) copy-start(u32[256]{0:T(256)} %constant.123) | copy-start | bytes 3076
  48.4 12.6 %copy-start.1 = (bf16[256,1024]{1,0:T(8,128)(2,1)S(1)}, bf16[256,1024]{1,0:T(8,128)(2,1)}, u32[]{:S(2)}) copy-start(bf16[256,1024]{1,0:T(8,128)(2,1)} %param.14) | copy-start | bytes 1572868
  48.4 13.1 %copy-start.6 = (bf16[256,1024]{1,0:T(8,128)(2,1)S(1)}, bf16[256,1024]{1,0:T(8,128)(2,1)}, u32[]{:S(2)}) copy-start(bf16[256,1024]{1,0:T(8,128)(2,1)} %param.15) | copy-start | bytes 1572868
  48.4 74.8 %all-to-all-start.1 = ((bf16[32,256,256]{1,2,0:T(8,128)(2,1)}), bf16[32,256,256]{1,2,0:T(8,128)(2,1)}, u32[]{:S(2)}, u32[]{:S(2)}) async-start(bf16[32,256,256]{1,2,0:T(8,128)(2,1)} %stack.5), calls=%async_computation.1 | async-start | bytes 8388608 | tf_op jit(solution)/shard_map/all_to_all | solution.py:149
  55.9 64.9 %all-gather.7.cloned.1.call-start = ((), (), s32[]{:S(2)}) async-start(), calls=%async_computation.4 | async-start | bytes 1310720 | tf_op jit(solution)/shard_map/all_gather | solution.py:24
  61.1 59.5 %copy-start.2 = (bf16[256,1024]{0,1:T(8,128)(2,1)}, bf16[256,1024]{0,1:T(8,128)(2,1)S(1)}, u32[]{:S(2)}) copy-start(bf16[256,1024]{0,1:T(8,128)(2,1)S(1)} %copy.119) | copy-start | bytes 1572868
  64.9 155.2 %all-gather.9.cloned.1.call-start = ((), (), s32[]{:S(2)}) async-start(), calls=%async_computation.5 | async-start | bytes 1310720 | tf_op jit(solution)/shard_map/all_gather | solution.py:24
  216.6 18.3 %all-to-all-start.3 = ((bf16[8,32,1024]{2,1,0:T(8,128)(2,1)}), bf16[8,32,1024]{2,1,0:T(8,128)(2,1)S(1)}, u32[]{:S(2)}, u32[]{:S(2)}) async-start(bf16[8,32,1024]{2,1,0:T(8,128)(2,1)} %bitcast.74), calls=%async_computation.3 | async-start | bytes 1048576 | tf_op jit(solution)/shard_map/all_to_all | solution.py:164
  220.2 3.6 %copy-start.3 = (bf16[256,1024]{0,1:T(8,128)(2,1)S(1)}, bf16[256,1024]{0,1:T(8,128)(2,1)}, u32[]{:S(2)}) copy-start(bf16[256,1024]{0,1:T(8,128)(2,1)} %copy-done.2) | copy-start | bytes 1572868
  223.8 2.4 %copy-start.5 = (f32[1024]{0:T(1024)S(1)}, f32[1024]{0:T(1024)}, u32[]{:S(2)}) copy-start(f32[1024]{0:T(1024)} %param.17) | copy-start | bytes 12292
Sparse Core Ops, SparseCore 0:
  65.0 48.0 all-gather.6
  123.3 22.1 all-gather.8
